TPU v7x, 32 devices: a whole 2x2x4 slice. The times are simulated.
32 devices in a mesh: layer: 8 (over z, x), row: 4 (over y, core).
Axes of the slice: x: 2, y: 2, z: 4, core: 2. Of those that a mesh axis runs over, the one named last changes fastest.
Arguments:
- right_side: float32 [8, 1024, 256], P('layer', 'row'), may hold values from -6 to 6
- reduce_factors: float32 [3, 8, 2, 1024, 1024], P(None, 'layer', None, 'row'), may hold values from -0.1875 to 0.1875
- solve_factors: float32 [8, 3, 1024, 1024], P('layer', None, 'row'), may hold values from -0.1875 to 0.1875
Outputs:
- solution: float32 [8, 1024, 256], P('layer', 'row')
All inputs are finite; a program needn't handle non-finite values.
Results may differ from a plain program's by a relative error of at most 0.00016.
Values sent between devices are 32-bit elements; how exact they have to be, the bound alone decides.
No kernel may reach another device: no remote copies, remote signals or barrier semaphores. Data moves between devices by JAX's collectives and lax.ppermute only.
A program may use at most 64 MiB of HBM per device.

v0:
```python
import jax
import jax.numpy as jnp
from jax import lax
from jax.sharding import PartitionSpec as P


def from_behind(shard, axis, by):
    devices = lax.axis_size(axis)
    pairs = [(i, i + by) for i in range(devices) if 0 <= i + by < devices]
    return lax.ppermute(shard, axis, pairs)


def product_of(left, right):
    return jnp.dot(left, right, precision=lax.Precision.HIGHEST, preferred_element_type=jnp.float32)


def neighbour_terms(vectors, left_mats, right_mats, stride):
    whole = lax.all_gather(vectors, "row", axis=1, tiled=True)
    lower = from_behind(whole, "layer", stride)
    upper = from_behind(whole, "layer", -stride)
    return (product_of(left_mats[0], lower[0]) + product_of(right_mats[0], upper[0]))[None]


def on_device(right_side, reduce_factors, solve_factors):
    layer_index = lax.axis_index("layer")
    level_count = reduce_factors.shape[0]
    current = right_side
    saved = right_side
    for level_index in range(level_count):
        stride = 1 << level_index
        terms = neighbour_terms(
            current, reduce_factors[level_index, :, 0], reduce_factors[level_index, :, 1], stride
        )
        saved = jnp.where(layer_index % (2 * stride) == stride, current, saved)
        current = jnp.where(layer_index % (2 * stride) == 0, current - terms, current)
    saved = jnp.where(layer_index == 0, current, saved)
    own_inverse = solve_factors[0, 0]
    base = product_of(own_inverse, lax.all_gather(saved, "row", axis=1, tiled=True)[0])[None]
    solution = jnp.where(layer_index == 0, base, jnp.zeros_like(base))
    for level_index in reversed(range(level_count)):
        stride = 1 << level_index
        terms = neighbour_terms(solution, solve_factors[:, 1], solve_factors[:, 2], stride)
        solution = jnp.where(layer_index % (2 * stride) == stride, base - terms, solution)
    return solution


def solution(mesh):
    placed = (
        P("layer", "row", None),
        P(None, "layer", None, "row", None),
        P("layer", None, "row", None),
    )
    return jax.shard_map(
        on_device, mesh=mesh, in_specs=placed, out_specs=P("layer", "row", None), check_vma=False
    )
```

profile of v0, /device:TPU:8, one launch (start us, length us, event | category | flops | bytes accessed | tf_op | source)
XLA Modules:
  0.0 427.2 jit_solution(3660228800837578581)
XLA Ops:
  6.5 0.7 all-gather.11.cloned.1.call-update
  7.3 19.5 %all-gather.11.cloned.1.call-done = f32[1,1024,256]{2,1,0:T(8,128)} async-done(((f32[1,256,256]{2,1,0:T(8,128)}), f32[1,1024,256]{2,1,0:T(8,128)}) %all-gather.11.cloned.1.call-update) | async-done | bytes 1048592 | tf_op jit(solution)/shard_map/all_gather | solution.py:18
  26.8 3.3 collective-permute-start.1
  30.2 2.5 collective-permute-start
  32.7 44.0 %collective-permute-done.1 = f32[1,1024,256]{2,1,0:T(8,128)S(1)} collective-permute-done((f32[1,1024,256]{2,1,0:T(8,128)}, f32[1,1024,256]{2,1,0:T(8,128)S(1)}, u32[]{:S(2)}, u32[]{:S(2)}) %collective-permute-start.1) | collective-permute-done | bytes 1048608 | tf_op jit(solution)/shard_map/ppermute | solution.py:10
  76.7 2.2 fusion.48
  79.0 3.0 fusion.14
  82.0 0.0 all-gather.15.cloned.1.call-start
  82.0 15.9 %all-gather.13.cloned.1.call-done = f32[1,1024,256]{2,1,0:T(8,128)} async-done(((f32[1,256,256]{2,1,0:T(8,128)}), f32[1,1024,256]{2,1,0:T(8,128)}) %all-gather.13.cloned.1.call-update) | async-done | bytes 1048592 | tf_op jit(solution)/shard_map/all_gather | solution.py:18
  98.0 2.4 collective-permute-start.3
  100.4 3.4 collective-permute-start.2
  103.8 21.5 %collective-permute-done.3 = f32[1,1024,256]{2,1,0:T(8,128)S(1)} collective-permute-done((f32[1,1024,256]{2,1,0:T(8,128)}, f32[1,1024,256]{2,1,0:T(8,128)S(1)}, u32[]{:S(2)}, u32[]{:S(2)}) %collective-permute-start.3) | collective-permute-done | bytes 1048608 | tf_op jit(solution)/shard_map/ppermute | solution.py:10
  125.4 2.3 fusion.43
  127.7 3.1 fusion.16
  130.8 0.0 all-gather.17.cloned.1.call-start
  130.8 16.7 %all-gather.15.cloned.1.call-done = f32[1,1024,256]{2,1,0:T(8,128)} async-done(((f32[1,256,256]{2,1,0:T(8,128)}), f32[1,1024,256]{2,1,0:T(8,128)}) %all-gather.15.cloned.1.call-update) | async-done | bytes 1048592 | tf_op jit(solution)/shard_map/all_gather | solution.py:18
  147.5 1.3 collective-permute-start.5
  148.8 7.4 %collective-permute-start.4 = (f32[1,1024,256]{2,1,0:T(8,128)}, f32[1,1024,256]{2,1,0:T(8,128)}, u32[]{:S(2)}, u32[]{:S(2)}) collective-permute-start(f32[1,1024,256]{2,1,0:T(8,128)} %all-gather.15.cloned.1.call-done), channel_id=1, source_target_pairs={{0,16},{4,20},{8,24},{12,28},{1,17},{5,21},{9,25},{13,29},{2,18},{... | collective-permute-start | bytes 3145736 | tf_op jit(solution)/shard_map/ppermute | solution.py:10
  156.2 19.8 %collective-permute-done.5 = f32[1,1024,256]{2,1,0:T(8,128)} collective-permute-done((f32[1,1024,256]{2,1,0:T(8,128)}, f32[1,1024,256]{2,1,0:T(8,128)}, u32[]{:S(2)}, u32[]{:S(2)}) %collective-permute-start.5) | collective-permute-done | bytes 1048608 | tf_op jit(solution)/shard_map/ppermute | solution.py:10
  176.0 2.6 fusion.38
  178.6 21.9 %collective-permute-done.4 = f32[1,1024,256]{2,1,0:T(8,128)} collective-permute-done((f32[1,1024,256]{2,1,0:T(8,128)}, f32[1,1024,256]{2,1,0:T(8,128)}, u32[]{:S(2)}, u32[]{:S(2)}) %collective-permute-start.4) | collective-permute-done | bytes 1048608 | tf_op jit(solution)/shard_map/ppermute | solution.py:10
  200.5 3.4 fusion.19
  203.9 0.0 all-gather.19.cloned.1.call-start
  204.0 17.9 %all-gather.17.cloned.1.call-done = f32[1,1024,256]{2,1,0:T(8,128)} async-done(((f32[1,256,256]{2,1,0:T(8,128)}), f32[1,1024,256]{2,1,0:T(8,128)}) %all-gather.17.cloned.1.call-update) | async-done | bytes 1048592 | tf_op jit(solution)/shard_map/all_gather | solution.py:38
  221.9 3.0 fusion.35
  224.9 0.7 select_bitcast_fusion
  225.7 16.8 %all-gather.19.cloned.1.call-done = f32[1024,256]{0,1:T(8,128)} async-done(((f32[256,256]{0,1:T(8,128)}), f32[1024,256]{0,1:T(8,128)}) %all-gather.19.cloned.1.call-update) | async-done | bytes 1048592 | tf_op jit(solution)/shard_map/all_gather | solution.py:18
  242.5 1.3 collective-permute-start.7
  243.8 5.6 %collective-permute-start.6 = (f32[1,1024,256]{1,2,0:T(8,128)}, f32[1,1024,256]{1,2,0:T(8,128)S(1)}, u32[]{:S(2)}, u32[]{:S(2)}) collective-permute-start(f32[1,1024,256]{1,2,0:T(8,128)} %bitcast.122), channel_id=1, source_target_pairs={{0,16},{4,20},{8,24},{12,28},{1,17},{5,21},{9,25},{13,29},{2,18},{... | collective-permute-start | bytes 3145736 | tf_op jit(solution)/shard_map/ppermute | solution.py:10
  249.4 21.5 %collective-permute-done.7 = f32[1,1024,256]{1,2,0:T(8,128)S(1)} collective-permute-done((f32[1,1024,256]{1,2,0:T(8,128)}, f32[1,1024,256]{1,2,0:T(8,128)S(1)}, u32[]{:S(2)}, u32[]{:S(2)}) %collective-permute-start.7) | collective-permute-done | bytes 1048608 | tf_op jit(solution)/shard_map/ppermute | solution.py:10
  270.9 1.0 fusion.28
  272.0 22.7 %collective-permute-done.6 = f32[1,1024,256]{1,2,0:T(8,128)S(1)} collective-permute-done((f32[1,1024,256]{1,2,0:T(8,128)}, f32[1,1024,256]{1,2,0:T(8,128)S(1)}, u32[]{:S(2)}, u32[]{:S(2)}) %collective-permute-start.6) | collective-permute-done | bytes 1048608 | tf_op jit(solution)/shard_map/ppermute | solution.py:10
  294.6 1.7 fusion.9
  296.4 0.2 all-gather.23.cloned.1.call-start
  296.6 17.5 %all-gather.21.cloned.1.call-done = f32[1024,256]{0,1:T(8,128)} async-done(((f32[256,256]{0,1:T(8,128)}), f32[1024,256]{0,1:T(8,128)}) %all-gather.21.cloned.1.call-update) | async-done | bytes 1048592 | tf_op jit(solution)/shard_map/all_gather | solution.py:18
  314.1 2.4 collective-permute-start.9
  316.6 3.4 collective-permute-start.8
  320.0 21.5 %collective-permute-done.9 = f32[1,1024,256]{1,2,0:T(8,128)S(1)} collective-permute-done((f32[1,1024,256]{1,2,0:T(8,128)}, f32[1,1024,256]{1,2,0:T(8,128)S(1)}, u32[]{:S(2)}, u32[]{:S(2)}) %collective-permute-start.9) | collective-permute-done | bytes 1048608 | tf_op jit(solution)/shard_map/ppermute | solution.py:10
  341.5 1.0 fusion.23
  342.6 1.1 collective-permute-done.8
  343.7 1.7 fusion.6
  345.5 17.9 %all-gather.23.cloned.1.call-done = f32[1024,256]{0,1:T(8,128)} async-done(((f32[256,256]{0,1:T(8,128)}), f32[1024,256]{0,1:T(8,128)}) %all-gather.23.cloned.1.call-update) | async-done | bytes 1048592 | tf_op jit(solution)/shard_map/all_gather | solution.py:18
  363.4 3.3 collective-permute-start.11
  366.7 2.5 collective-permute-start.10
  369.2 44.1 %collective-permute-done.11 = f32[1,1024,256]{1,2,0:T(8,128)} collective-permute-done((f32[1,1024,256]{1,2,0:T(8,128)}, f32[1,1024,256]{1,2,0:T(8,128)}, u32[]{:S(2)}, u32[]{:S(2)}) %collective-permute-start.11) | collective-permute-done | bytes 1048608 | tf_op jit(solution)/shard_map/ppermute | solution.py:10
  413.3 2.3 fusion.20
  415.6 3.0 fusion.3
  418.6 1.8 copy.8
  (16 shorter events, 0.2 us)
Async XLA Ops:
  6.5 20.3 %all-gather.11.cloned.1.call-start = ((), (), s32[]{:S(2)}) async-start(), calls=%async_computation | async-start | bytes 1310720 | tf_op jit(solution)/shard_map/all_gather | solution.py:18
  7.3 90.7 %all-gather.13.cloned.1.call-start = ((), (), s32[]{:S(2)}) async-start(), calls=%async_computation.1 | async-start | bytes 1310720 | tf_op jit(solution)/shard_map/all_gather | solution.py:18
  26.8 49.9 %collective-permute-start.1 = (f32[1,1024,256]{2,1,0:T(8,128)}, f32[1,1024,256]{2,1,0:T(8,128)S(1)}, u32[]{:S(2)}, u32[]{:S(2)}) collective-permute-start(f32[1,1024,256]{2,1,0:T(8,128)} %all-gather.11.cloned.1.call-done), channel_id=1, source_target_pairs={{4,0},{8,4},{12,8},{16,12},{20,16},{24,20},{28,24},{5,1},{9,5},{13... | collective-permute-start | bytes 3145736 | tf_op jit(solution)/shard_map/ppermute | solution.py:10
  30.2 48.8 %collective-permute-start = (f32[1,1024,256]{2,1,0:T(8,128)}, f32[1,1024,256]{2,1,0:T(8,128)S(1)}, u32[]{:S(2)}, u32[]{:S(2)}) collective-permute-start(f32[1,1024,256]{2,1,0:T(8,128)} %all-gather.11.cloned.1.call-done), channel_id=1, source_target_pairs={{0,4},{4,8},{8,12},{12,16},{16,20},{20,24},{24,28},{1,5},{5,9},{9,... | collective-permute-start | bytes 3145736 | tf_op jit(solution)/shard_map/ppermute | solution.py:10
  82.0 65.5 %all-gather.15.cloned.1.call-start = ((), (), s32[]{:S(2)}) async-start(), calls=%async_computation.2 | async-start | bytes 1310720 | tf_op jit(solution)/shard_map/all_gather | solution.py:18
  98.0 27.4 %collective-permute-start.3 = (f32[1,1024,256]{2,1,0:T(8,128)}, f32[1,1024,256]{2,1,0:T(8,128)S(1)}, u32[]{:S(2)}, u32[]{:S(2)}) collective-permute-start(f32[1,1024,256]{2,1,0:T(8,128)} %all-gather.13.cloned.1.call-done), channel_id=1, source_target_pairs={{8,0},{12,4},{16,8},{20,12},{24,16},{28,20},{9,1},{13,5},{17,9},{2... | collective-permute-start | bytes 3145736 | tf_op jit(solution)/shard_map/ppermute | solution.py:10
  100.4 27.3 %collective-permute-start.2 = (f32[1,1024,256]{2,1,0:T(8,128)}, f32[1,1024,256]{2,1,0:T(8,128)S(1)}, u32[]{:S(2)}, u32[]{:S(2)}) collective-permute-start(f32[1,1024,256]{2,1,0:T(8,128)} %all-gather.13.cloned.1.call-done), channel_id=1, source_target_pairs={{0,8},{4,12},{8,16},{12,20},{16,24},{20,28},{1,9},{5,13},{9,17},{1... | collective-permute-start | bytes 3145736 | tf_op jit(solution)/shard_map/ppermute | solution.py:10
  127.6 72.9 %copy-start.1 = (f32[1,256,256]{2,1,0:T(8,128)S(1)}, f32[1,256,256]{2,1,0:T(8,128)}, u32[]{:S(2)}) copy-start(f32[1,256,256]{2,1,0:T(8,128)} %fusion.14) | copy-start | bytes 786436
  130.7 91.1 %copy-start = (f32[1,3,256,1024]{3,2,1,0:T(8,128)S(1)}, f32[1,3,256,1024]{3,2,1,0:T(8,128)}, u32[]{:S(2)}) copy-start(f32[1,3,256,1024]{3,2,1,0:T(8,128)} %param.5) | copy-start | bytes 9437188
  130.8 91.1 %all-gather.17.cloned.1.call-start = ((), (), s32[]{:S(2)}) async-start(), calls=%async_computation.3 | async-start | bytes 1310720 | tf_op jit(solution)/shard_map/all_gather | solution.py:38
  147.5 28.5 %collective-permute-start.5 = (f32[1,1024,256]{2,1,0:T(8,128)}, f32[1,1024,256]{2,1,0:T(8,128)}, u32[]{:S(2)}, u32[]{:S(2)}) collective-permute-start(f32[1,1024,256]{2,1,0:T(8,128)} %all-gather.15.cloned.1.call-done), channel_id=1, source_target_pairs={{16,0},{20,4},{24,8},{28,12},{17,1},{21,5},{25,9},{29,13},{18,2},{... | collective-permute-start | bytes 3145736 | tf_op jit(solution)/shard_map/ppermute | solution.py:10
  148.8 51.7 %collective-permute-start.4 = (f32[1,1024,256]{2,1,0:T(8,128)}, f32[1,1024,256]{2,1,0:T(8,128)}, u32[]{:S(2)}, u32[]{:S(2)}) collective-permute-start(f32[1,1024,256]{2,1,0:T(8,128)} %all-gather.15.cloned.1.call-done), channel_id=1, source_target_pairs={{0,16},{4,20},{8,24},{12,28},{1,17},{5,21},{9,25},{13,29},{2,18},{... | collective-permute-start | bytes 3145736 | tf_op jit(solution)/shard_map/ppermute | solution.py:10
  203.9 38.6 %all-gather.19.cloned.1.call-start = ((), (), s32[]{:S(2)}) async-start(), calls=%async_computation.4 | async-start | bytes 1310720 | tf_op jit(solution)/shard_map/all_gather | solution.py:18
  225.7 88.5 %all-gather.21.cloned.1.call-start = ((), (), s32[]{:S(2)}) async-start(), calls=%async_computation.5 | async-start | bytes 1310720 | tf_op jit(solution)/shard_map/all_gather | solution.py:18
  242.5 28.4 %collective-permute-start.7 = (f32[1,1024,256]{1,2,0:T(8,128)}, f32[1,1024,256]{1,2,0:T(8,128)S(1)}, u32[]{:S(2)}, u32[]{:S(2)}) collective-permute-start(f32[1,1024,256]{1,2,0:T(8,128)} %bitcast.121), channel_id=1, source_target_pairs={{16,0},{20,4},{24,8},{28,12},{17,1},{21,5},{25,9},{29,13},{18,2},{... | collective-permute-start | bytes 3145736 | tf_op jit(solution)/shard_map/ppermute | solution.py:10
  243.8 50.8 %collective-permute-start.6 = (f32[1,1024,256]{1,2,0:T(8,128)}, f32[1,1024,256]{1,2,0:T(8,128)S(1)}, u32[]{:S(2)}, u32[]{:S(2)}) collective-permute-start(f32[1,1024,256]{1,2,0:T(8,128)} %bitcast.122), channel_id=1, source_target_pairs={{0,16},{4,20},{8,24},{12,28},{1,17},{5,21},{9,25},{13,29},{2,18},{... | collective-permute-start | bytes 3145736 | tf_op jit(solution)/shard_map/ppermute | solution.py:10
  296.4 67.0 %all-gather.23.cloned.1.call-start = ((), (), s32[]{:S(2)}) async-start(), calls=%async_computation.6 | async-start | bytes 1310720 | tf_op jit(solution)/shard_map/all_gather | solution.py:18
  314.1 27.4 %collective-permute-start.9 = (f32[1,1024,256]{1,2,0:T(8,128)}, f32[1,1024,256]{1,2,0:T(8,128)S(1)}, u32[]{:S(2)}, u32[]{:S(2)}) collective-permute-start(f32[1,1024,256]{1,2,0:T(8,128)} %bitcast.125), channel_id=1, source_target_pairs={{8,0},{12,4},{16,8},{20,12},{24,16},{28,20},{9,1},{13,5},{17,9},{2... | collective-permute-start | bytes 3145736 | tf_op jit(solution)/shard_map/ppermute | solution.py:10
  316.6 27.1 %collective-permute-start.8 = (f32[1,1024,256]{1,2,0:T(8,128)}, f32[1,1024,256]{1,2,0:T(8,128)S(1)}, u32[]{:S(2)}, u32[]{:S(2)}) collective-permute-start(f32[1,1024,256]{1,2,0:T(8,128)} %bitcast.126), channel_id=1, source_target_pairs={{0,8},{4,12},{8,16},{12,20},{16,24},{20,28},{1,9},{5,13},{9,17},{1... | collective-permute-start | bytes 3145736 | tf_op jit(solution)/shard_map/ppermute | solution.py:10
  363.4 50.0 %collective-permute-start.11 = (f32[1,1024,256]{1,2,0:T(8,128)}, f32[1,1024,256]{1,2,0:T(8,128)}, u32[]{:S(2)}, u32[]{:S(2)}) collective-permute-start(f32[1,1024,256]{1,2,0:T(8,128)} %bitcast.123), channel_id=1, source_target_pairs={{4,0},{8,4},{12,8},{16,12},{20,16},{24,20},{28,24},{5,1},{9,5},{13... | collective-permute-start | bytes 3145736 | tf_op jit(solution)/shard_map/ppermute | solution.py:10
  366.7 48.9 %collective-permute-start.10 = (f32[1,1024,256]{1,2,0:T(8,128)}, f32[1,1024,256]{1,2,0:T(8,128)}, u32[]{:S(2)}, u32[]{:S(2)}) collective-permute-start(f32[1,1024,256]{1,2,0:T(8,128)} %bitcast.124), channel_id=1, source_target_pairs={{0,4},{4,8},{8,12},{12,16},{16,20},{20,24},{24,28},{1,5},{5,9},{9,... | collective-permute-start | bytes 3145736 | tf_op jit(solution)/shard_map/ppermute | solution.py:10
Sparse Core Ops, SparseCore 0:
  8.9 17.8 all-gather.10
  82.1 15.8 all-gather.12
  130.9 16.5 all-gather.14
  204.0 17.7 all-gather.16
  225.8 16.7 all-gather.18
  296.5 17.5 all-gather.20
  345.6 17.7 all-gather.22
where the time goes:
time: 428 us; the launch traced here: 427 us
  waiting for transfers between devices  341 us (80%)
  starting transfers between devices  39.3 us (9%)
  matrix products  30.4 us (7%)
  between operations  13.7 us (3%)
    ppermute x12, waiting for transfers between devices, from_behind(): return lax.ppermute(shard, axis, pairs)  218 us
    all_gather x6, waiting for transfers between devices, neighbour_terms(): whole = lax.all_gather(vectors, 'row', axis=1, tiled=True)  104 us
    ppermute x12, starting transfers between devices, from_behind(): return lax.ppermute(shard, axis, pairs)  38.9 us
    dot_general x13, matrix products, product_of(): jnp.dot(left, right, precision=lax.Precision.HIGHEST, preferred_element_t...  30.4 us
    all_gather x1, waiting for transfers between devices, on_device(): lax.all_gather(saved, 'row', axis=1, tiled=True)[0]  17.9 us
  transfers between devices with their start and end apart: 19, of which 16 were waited for; matrix products, arithmetic and copies ran while one was open for 3% of the time, Pallas kernels for 0%

commit v1 on v0

--- a/solution.py
+++ b/solution.py
@@ -35,7 +35,12 @@
         current = jnp.where(layer_index % (2 * stride) == 0, current - terms, current)
     saved = jnp.where(layer_index == 0, current, saved)
     own_inverse = solve_factors[0, 0]
-    base = product_of(own_inverse, lax.all_gather(saved, "row", axis=1, tiled=True)[0])[None]
+    base = product_of(
+        own_inverse,
+        jnp.concatenate(
+            lax.all_to_all(jnp.stack([saved] * lax.axis_size("row")), "row", 0, 0), axis=1
+        )[0],
+    )[None]
     solution = jnp.where(layer_index == 0, base, jnp.zeros_like(base))
     for level_index in reversed(range(level_count)):
         stride = 1 << level_index

time: 428 us -> 425 us (level)
  blocking collectives: 0 us -> 16.9 us
  waiting for transfers between devices: 341 us -> 325 us
    all_gather x1 -> x0, waiting for transfers between devices: 17.9 us -> none  [on_device(): lax.all_gather(saved, 'row', axis=1, tiled=True)[0]]
    all_to_all x0 -> x1, blocking collectives: none -> 16.9 us  [on_device(): lax.all_to_all(jnp.stack([saved] * lax.axis_size('row')), 'row', 0, 0)]
  transfers between devices with their start and end apart: 19 -> 18, of which waited for: 16 -> 15; matrix products, arithmetic and copies ran while one was open for 3% -> 3% of each run, Pallas kernels for 0% -> 0%
where the time goes in v1:
time: 425 us; the launch traced here: 424 us
  waiting for transfers between devices  325 us (76%)
  starting transfers between devices  38.3 us (9%)
  matrix products  28.2 us (7%)
  blocking collectives  16.9 us (4%)
  between operations  13.7 us (3%)
    ppermute x12, waiting for transfers between devices, from_behind(): return lax.ppermute(shard, axis, pairs)  218 us
    all_gather x6, waiting for transfers between devices, neighbour_terms(): whole = lax.all_gather(vectors, 'row', axis=1, tiled=True)  106 us
    ppermute x12, starting transfers between devices, from_behind(): return lax.ppermute(shard, axis, pairs)  38.1 us
    dot_general x13, matrix products, product_of(): jnp.dot(left, right, precision=lax.Precision.HIGHEST, preferred_element_t...  28.2 us
    all_to_all x1, blocking collectives, on_device(): lax.all_to_all(jnp.stack([saved] * lax.axis_size('row')), 'row', 0, 0)  16.9 us
  transfers between devices with their start and end apart: 18, of which 15 were waited for; matrix products, arithmetic and copies ran while one was open for 3% of the time, Pallas kernels for 0%

profile of v1, /device:TPU:8, one launch (start us, length us, event | category | flops | bytes accessed | tf_op | source)
XLA Modules:
  0.0 424.5 jit_solution(3235455694539176135)
XLA Ops:
  6.5 0.7 all-gather.10.cloned.1.call-update
  7.3 19.5 %all-gather.10.cloned.1.call-done = f32[1,1024,256]{2,1,0:T(8,128)} async-done(((f32[1,256,256]{2,1,0:T(8,128)}), f32[1,1024,256]{2,1,0:T(8,128)}) %all-gather.10.cloned.1.call-update) | async-done | bytes 1048592 | tf_op jit(solution)/shard_map/all_gather | solution.py:18
  26.8 3.3 collective-permute-start.1
  30.2 2.5 collective-permute-start
  32.7 44.0 %collective-permute-done.1 = f32[1,1024,256]{2,1,0:T(8,128)S(1)} collective-permute-done((f32[1,1024,256]{2,1,0:T(8,128)}, f32[1,1024,256]{2,1,0:T(8,128)S(1)}, u32[]{:S(2)}, u32[]{:S(2)}) %collective-permute-start.1) | collective-permute-done | bytes 1048608 | tf_op jit(solution)/shard_map/ppermute | solution.py:10
  76.7 2.2 fusion.48
  79.0 3.0 fusion.14
  82.0 0.0 all-gather.14.cloned.1.call-start
  82.0 15.9 %all-gather.12.cloned.1.call-done = f32[1,1024,256]{2,1,0:T(8,128)} async-done(((f32[1,256,256]{2,1,0:T(8,128)}), f32[1,1024,256]{2,1,0:T(8,128)}) %all-gather.12.cloned.1.call-update) | async-done | bytes 1048592 | tf_op jit(solution)/shard_map/all_gather | solution.py:18
  98.0 2.4 collective-permute-start.3
  100.4 3.4 collective-permute-start.2
  103.8 21.5 %collective-permute-done.3 = f32[1,1024,256]{2,1,0:T(8,128)S(1)} collective-permute-done((f32[1,1024,256]{2,1,0:T(8,128)}, f32[1,1024,256]{2,1,0:T(8,128)S(1)}, u32[]{:S(2)}, u32[]{:S(2)}) %collective-permute-start.3) | collective-permute-done | bytes 1048608 | tf_op jit(solution)/shard_map/ppermute | solution.py:10
  125.4 2.3 fusion.43
  127.7 3.1 fusion.16
  130.8 0.0 all-gather.16.cloned.1.call-start
  130.8 16.7 %all-gather.14.cloned.1.call-done = f32[1,1024,256]{2,1,0:T(8,128)} async-done(((f32[1,256,256]{2,1,0:T(8,128)}), f32[1,1024,256]{2,1,0:T(8,128)}) %all-gather.14.cloned.1.call-update) | async-done | bytes 1048592 | tf_op jit(solution)/shard_map/all_gather | solution.py:18
  147.5 1.3 collective-permute-start.5
  148.8 6.5 %collective-permute-start.4 = (f32[1,1024,256]{2,1,0:T(8,128)}, f32[1,1024,256]{2,1,0:T(8,128)}, u32[]{:S(2)}, u32[]{:S(2)}) collective-permute-start(f32[1,1024,256]{2,1,0:T(8,128)} %all-gather.14.cloned.1.call-done), channel_id=1, source_target_pairs={{0,16},{4,20},{8,24},{12,28},{1,17},{5,21},{9,25},{13,29},{2,18},{... | collective-permute-start | bytes 3145736 | tf_op jit(solution)/shard_map/ppermute | solution.py:10
  155.3 20.6 %collective-permute-done.5 = f32[1,1024,256]{2,1,0:T(8,128)S(1)} collective-permute-done((f32[1,1024,256]{2,1,0:T(8,128)}, f32[1,1024,256]{2,1,0:T(8,128)S(1)}, u32[]{:S(2)}, u32[]{:S(2)}) %collective-permute-start.5) | collective-permute-done | bytes 1048608 | tf_op jit(solution)/shard_map/ppermute | solution.py:10
  175.9 2.3 fusion.38
  178.2 21.4 %collective-permute-done.4 = f32[1,1024,256]{2,1,0:T(8,128)} collective-permute-done((f32[1,1024,256]{2,1,0:T(8,128)}, f32[1,1024,256]{2,1,0:T(8,128)}, u32[]{:S(2)}, u32[]{:S(2)}) %collective-permute-start.4) | collective-permute-done | bytes 1048608 | tf_op jit(solution)/shard_map/ppermute | solution.py:10
  199.6 2.7 fusion.20
  202.3 0.1 stack.2
  202.4 16.9 %all_to_all.5 = f32[4,1,256,256]{3,2,1,0:T(8,128)S(1)} all-to-all(f32[4,1,256,256]{3,2,1,0:T(8,128)S(1)} %stack.2), channel_id=1, replica_groups=mesh['layer'=8,'row'=4] {'row'}, dimensions={0} | all-to-all | bytes 2097152 | tf_op jit(solution)/shard_map/all_to_all | solution.py:41
  219.3 1.8 fusion.36
  221.1 0.7 select_bitcast_fusion
  221.8 0.0 all-gather.18.cloned.1.call-start
  221.9 17.9 %all-gather.16.cloned.1.call-done = f32[1024,256]{0,1:T(8,128)} async-done(((f32[256,256]{0,1:T(8,128)}), f32[1024,256]{0,1:T(8,128)}) %all-gather.16.cloned.1.call-update) | async-done | bytes 1048592 | tf_op jit(solution)/shard_map/all_gather | solution.py:18
  239.8 1.3 collective-permute-start.7
  241.0 5.8 %collective-permute-start.6 = (f32[1,1024,256]{1,2,0:T(8,128)}, f32[1,1024,256]{1,2,0:T(8,128)S(1)}, u32[]{:S(2)}, u32[]{:S(2)}) collective-permute-start(f32[1,1024,256]{1,2,0:T(8,128)} %bitcast.126), channel_id=1, source_target_pairs={{0,16},{4,20},{8,24},{12,28},{1,17},{5,21},{9,25},{13,29},{2,18},{... | collective-permute-start | bytes 3145736 | tf_op jit(solution)/shard_map/ppermute | solution.py:10
  246.8 21.3 %collective-permute-done.7 = f32[1,1024,256]{1,2,0:T(8,128)S(1)} collective-permute-done((f32[1,1024,256]{1,2,0:T(8,128)}, f32[1,1024,256]{1,2,0:T(8,128)S(1)}, u32[]{:S(2)}, u32[]{:S(2)}) %collective-permute-start.7) | collective-permute-done | bytes 1048608 | tf_op jit(solution)/shard_map/ppermute | solution.py:10
  268.1 1.0 fusion.29
  269.2 22.7 %collective-permute-done.6 = f32[1,1024,256]{1,2,0:T(8,128)S(1)} collective-permute-done((f32[1,1024,256]{1,2,0:T(8,128)}, f32[1,1024,256]{1,2,0:T(8,128)S(1)}, u32[]{:S(2)}, u32[]{:S(2)}) %collective-permute-start.6) | collective-permute-done | bytes 1048608 | tf_op jit(solution)/shard_map/ppermute | solution.py:10
  291.8 1.7 fusion.9
  293.7 17.7 %all-gather.18.cloned.1.call-done = f32[1024,256]{0,1:T(8,128)} async-done(((f32[256,256]{0,1:T(8,128)}), f32[1024,256]{0,1:T(8,128)}) %all-gather.18.cloned.1.call-update) | async-done | bytes 1048592 | tf_op jit(solution)/shard_map/all_gather | solution.py:18
  311.4 2.4 collective-permute-start.9
  313.8 3.4 collective-permute-start.8
  317.2 21.5 %collective-permute-done.9 = f32[1,1024,256]{1,2,0:T(8,128)S(1)} collective-permute-done((f32[1,1024,256]{1,2,0:T(8,128)}, f32[1,1024,256]{1,2,0:T(8,128)S(1)}, u32[]{:S(2)}, u32[]{:S(2)}) %collective-permute-start.9) | collective-permute-done | bytes 1048608 | tf_op jit(solution)/shard_map/ppermute | solution.py:10
  338.8 1.0 fusion.24
  339.8 1.1 collective-permute-done.8
  340.9 1.8 fusion.6
  342.7 17.9 %all-gather.20.cloned.1.call-done = f32[1024,256]{0,1:T(8,128)} async-done(((f32[256,256]{0,1:T(8,128)}), f32[1024,256]{0,1:T(8,128)}) %all-gather.20.cloned.1.call-update) | async-done | bytes 1048592 | tf_op jit(solution)/shard_map/all_gather | solution.py:18
  360.6 3.3 collective-permute-start.11
  363.9 2.5 collective-permute-start.10
  366.4 44.1 %collective-permute-done.11 = f32[1,1024,256]{1,2,0:T(8,128)} collective-permute-done((f32[1,1024,256]{1,2,0:T(8,128)}, f32[1,1024,256]{1,2,0:T(8,128)}, u32[]{:S(2)}, u32[]{:S(2)}) %collective-permute-start.11) | collective-permute-done | bytes 1048608 | tf_op jit(solution)/shard_map/ppermute | solution.py:10
  410.6 2.3 fusion.21
  412.8 3.0 fusion.3
  415.8 1.8 copy.8
  (15 shorter events, 0.2 us)
Async XLA Ops:
  6.5 20.3 %all-gather.10.cloned.1.call-start = ((), (), s32[]{:S(2)}) async-start(), calls=%async_computation.1 | async-start | bytes 1310720 | tf_op jit(solution)/shard_map/all_gather | solution.py:18
  7.3 90.7 %all-gather.12.cloned.1.call-start = ((), (), s32[]{:S(2)}) async-start(), calls=%async_computation.2 | async-start | bytes 1310720 | tf_op jit(solution)/shard_map/all_gather | solution.py:18
  26.8 49.9 %collective-permute-start.1 = (f32[1,1024,256]{2,1,0:T(8,128)}, f32[1,1024,256]{2,1,0:T(8,128)S(1)}, u32[]{:S(2)}, u32[]{:S(2)}) collective-permute-start(f32[1,1024,256]{2,1,0:T(8,128)} %all-gather.10.cloned.1.call-done), channel_id=1, source_target_pairs={{4,0},{8,4},{12,8},{16,12},{20,16},{24,20},{28,24},{5,1},{9,5},{13... | collective-permute-start | bytes 3145736 | tf_op jit(solution)/shard_map/ppermute | solution.py:10
  30.2 48.8 %collective-permute-start = (f32[1,1024,256]{2,1,0:T(8,128)}, f32[1,1024,256]{2,1,0:T(8,128)S(1)}, u32[]{:S(2)}, u32[]{:S(2)}) collective-permute-start(f32[1,1024,256]{2,1,0:T(8,128)} %all-gather.10.cloned.1.call-done), channel_id=1, source_target_pairs={{0,4},{4,8},{8,12},{12,16},{16,20},{20,24},{24,28},{1,5},{5,9},{9,... | collective-permute-start | bytes 3145736 | tf_op jit(solution)/shard_map/ppermute | solution.py:10
  82.0 65.5 %all-gather.14.cloned.1.call-start = ((), (), s32[]{:S(2)}) async-start(), calls=%async_computation.3 | async-start | bytes 1310720 | tf_op jit(solution)/shard_map/all_gather | solution.py:18
  98.0 27.4 %collective-permute-start.3 = (f32[1,1024,256]{2,1,0:T(8,128)}, f32[1,1024,256]{2,1,0:T(8,128)S(1)}, u32[]{:S(2)}, u32[]{:S(2)}) collective-permute-start(f32[1,1024,256]{2,1,0:T(8,128)} %all-gather.12.cloned.1.call-done), channel_id=1, source_target_pairs={{8,0},{12,4},{16,8},{20,12},{24,16},{28,20},{9,1},{13,5},{17,9},{2... | collective-permute-start | bytes 3145736 | tf_op jit(solution)/shard_map/ppermute | solution.py:10
  100.4 27.3 %collective-permute-start.2 = (f32[1,1024,256]{2,1,0:T(8,128)}, f32[1,1024,256]{2,1,0:T(8,128)S(1)}, u32[]{:S(2)}, u32[]{:S(2)}) collective-permute-start(f32[1,1024,256]{2,1,0:T(8,128)} %all-gather.12.cloned.1.call-done), channel_id=1, source_target_pairs={{0,8},{4,12},{8,16},{12,20},{16,24},{20,28},{1,9},{5,13},{9,17},{1... | collective-permute-start | bytes 3145736 | tf_op jit(solution)/shard_map/ppermute | solution.py:10
  127.6 72.0 %copy-start.1 = (f32[1,256,256]{2,1,0:T(8,128)S(1)}, f32[1,256,256]{2,1,0:T(8,128)}, u32[]{:S(2)}) copy-start(f32[1,256,256]{2,1,0:T(8,128)} %fusion.14) | copy-start | bytes 786436
  130.8 109.0 %all-gather.16.cloned.1.call-start = ((), (), s32[]{:S(2)}) async-start(), calls=%async_computation.4 | async-start | bytes 1310720 | tf_op jit(solution)/shard_map/all_gather | solution.py:18
  147.5 28.4 %collective-permute-start.5 = (f32[1,1024,256]{2,1,0:T(8,128)}, f32[1,1024,256]{2,1,0:T(8,128)S(1)}, u32[]{:S(2)}, u32[]{:S(2)}) collective-permute-start(f32[1,1024,256]{2,1,0:T(8,128)} %all-gather.14.cloned.1.call-done), channel_id=1, source_target_pairs={{16,0},{20,4},{24,8},{28,12},{17,1},{21,5},{25,9},{29,13},{18,2},{... | collective-permute-start | bytes 3145736 | tf_op jit(solution)/shard_map/ppermute | solution.py:10
  148.8 50.8 %collective-permute-start.4 = (f32[1,1024,256]{2,1,0:T(8,128)}, f32[1,1024,256]{2,1,0:T(8,128)}, u32[]{:S(2)}, u32[]{:S(2)}) collective-permute-start(f32[1,1024,256]{2,1,0:T(8,128)} %all-gather.14.cloned.1.call-done), channel_id=1, source_target_pairs={{0,16},{4,20},{8,24},{12,28},{1,17},{5,21},{9,25},{13,29},{2,18},{... | collective-permute-start | bytes 3145736 | tf_op jit(solution)/shard_map/ppermute | solution.py:10
  178.2 41.0 %copy-start = (f32[1,3,256,1024]{3,2,1,0:T(8,128)S(1)}, f32[1,3,256,1024]{3,2,1,0:T(8,128)}, u32[]{:S(2)}) copy-start(f32[1,3,256,1024]{3,2,1,0:T(8,128)} %param.5) | copy-start | bytes 9437188
  221.8 89.5 %all-gather.18.cloned.1.call-start = ((), (), s32[]{:S(2)}) async-start(), calls=%async_computation.5 | async-start | bytes 1310720 | tf_op jit(solution)/shard_map/all_gather | solution.py:18
  239.8 28.4 %collective-permute-start.7 = (f32[1,1024,256]{1,2,0:T(8,128)}, f32[1,1024,256]{1,2,0:T(8,128)S(1)}, u32[]{:S(2)}, u32[]{:S(2)}) collective-permute-start(f32[1,1024,256]{1,2,0:T(8,128)} %bitcast.125), channel_id=1, source_target_pairs={{16,0},{20,4},{24,8},{28,12},{17,1},{21,5},{25,9},{29,13},{18,2},{... | collective-permute-start | bytes 3145736 | tf_op jit(solution)/shard_map/ppermute | solution.py:10
  241.0 50.8 %collective-permute-start.6 = (f32[1,1024,256]{1,2,0:T(8,128)}, f32[1,1024,256]{1,2,0:T(8,128)S(1)}, u32[]{:S(2)}, u32[]{:S(2)}) collective-permute-start(f32[1,1024,256]{1,2,0:T(8,128)} %bitcast.126), channel_id=1, source_target_pairs={{0,16},{4,20},{8,24},{12,28},{1,17},{5,21},{9,25},{13,29},{2,18},{... | collective-permute-start | bytes 3145736 | tf_op jit(solution)/shard_map/ppermute | solution.py:10
  293.6 67.0 %all-gather.20.cloned.1.call-start = ((), (), s32[]{:S(2)}) async-start(), calls=%async_computation.6 | async-start | bytes 1310720 | tf_op jit(solution)/shard_map/all_gather | solution.py:18
  311.4 27.4 %collective-permute-start.9 = (f32[1,1024,256]{1,2,0:T(8,128)}, f32[1,1024,256]{1,2,0:T(8,128)S(1)}, u32[]{:S(2)}, u32[]{:S(2)}) collective-permute-start(f32[1,1024,256]{1,2,0:T(8,128)} %bitcast.129), channel_id=1, source_target_pairs={{8,0},{12,4},{16,8},{20,12},{24,16},{28,20},{9,1},{13,5},{17,9},{2... | collective-permute-start | bytes 3145736 | tf_op jit(solution)/shard_map/ppermute | solution.py:10
  313.8 27.1 %collective-permute-start.8 = (f32[1,1024,256]{1,2,0:T(8,128)}, f32[1,1024,256]{1,2,0:T(8,128)S(1)}, u32[]{:S(2)}, u32[]{:S(2)}) collective-permute-start(f32[1,1024,256]{1,2,0:T(8,128)} %bitcast.130), channel_id=1, source_target_pairs={{0,8},{4,12},{8,16},{12,20},{16,24},{20,28},{1,9},{5,13},{9,17},{1... | collective-permute-start | bytes 3145736 | tf_op jit(solution)/shard_map/ppermute | solution.py:10
  360.6 50.0 %collective-permute-start.11 = (f32[1,1024,256]{1,2,0:T(8,128)}, f32[1,1024,256]{1,2,0:T(8,128)}, u32[]{:S(2)}, u32[]{:S(2)}) collective-permute-start(f32[1,1024,256]{1,2,0:T(8,128)} %bitcast.127), channel_id=1, source_target_pairs={{4,0},{8,4},{12,8},{16,12},{20,16},{24,20},{28,24},{5,1},{9,5},{13... | collective-permute-start | bytes 3145736 | tf_op jit(solution)/shard_map/ppermute | solution.py:10
  363.9 48.9 %collective-permute-start.10 = (f32[1,1024,256]{1,2,0:T(8,128)}, f32[1,1024,256]{1,2,0:T(8,128)}, u32[]{:S(2)}, u32[]{:S(2)}) collective-permute-start(f32[1,1024,256]{1,2,0:T(8,128)} %bitcast.128), channel_id=1, source_target_pairs={{0,4},{4,8},{8,12},{12,16},{16,20},{20,24},{24,28},{1,5},{5,9},{9,... | collective-permute-start | bytes 3145736 | tf_op jit(solution)/shard_map/ppermute | solution.py:10
Sparse Core Ops, SparseCore 0:
  8.9 17.8 all-gather.9
  82.1 15.8 all-gather.11
  130.9 16.5 all-gather.13
  221.9 17.7 all-gather.15
  293.7 17.5 all-gather.17
  342.8 17.7 all-gather.19
